TPU v7x, 32 devices: a whole 2x2x4 slice. The times are simulated.
32 devices in a mesh: rows: 8 (over y, x, core), cols: 4 (over z).
Axes of the slice: x: 2, y: 2, z: 4, core: 2. Of those that a mesh axis runs over, the one named last changes fastest.
Arguments:
- grads: bfloat16 [9216, 8192], P(('rows', 'cols')), may hold values from -6 to 6
- tests: float32 [64, 8192], P(None, 'cols'), may hold values from -6 to 6
Outputs:
- solution: float32 [64, 8192], P(None, 'cols')
- scores: float32 [64, 9216], P(None, ('rows', 'cols'))
All inputs are finite; a program needn't handle non-finite values.
Results may differ from a plain program's by a relative error of at most 0.0041.
Values may be sent and summed in bfloat16 or wider, within the bound.
A program may use at most 64 MiB of HBM per device.

v0:
```python
import jax
import jax.numpy as jnp
from jax import lax
from jax.sharding import PartitionSpec as P

damping = 0.5


def per_device(grads, tests):
    n_total = grads.shape[0] * lax.axis_size("rows") * lax.axis_size("cols")
    width = grads.shape[1]
    own = tests.shape[1]
    direction = lax.all_gather(tests, "cols", axis=1, tiled=True)
    norm_now = jnp.sum(direction * direction, axis=1)

    def project(d):
        return lax.dot_general(
            grads,
            d.astype(jnp.bfloat16),
            (((1,), (1,)), ((), ())),
            preferred_element_type=jnp.float32,
        )

    partial_value = lax.dot_general(
        project(direction).astype(jnp.bfloat16),
        grads,
        (((0,), (0,)), ((), ())),
        preferred_element_type=jnp.float32,
    )
    image = lax.psum(partial_value, ("rows", "cols")) / n_total + damping * direction
    alpha = norm_now / jnp.sum(direction * image, axis=1)
    solution = alpha[:, None] * direction
    residual = direction - alpha[:, None] * image
    norm_next = jnp.sum(residual * residual, axis=1)
    direction = residual + (norm_next / norm_now)[:, None] * direction
    proj = project(direction)
    curv = lax.psum(
        jnp.sum(proj * proj.astype(jnp.bfloat16).astype(jnp.float32), axis=0), ("rows", "cols")
    )
    curv = curv / n_total + damping * jnp.sum(direction * direction, axis=1)
    solution = solution + (norm_next / curv)[:, None] * direction
    scores = lax.dot_general(
        solution.astype(jnp.bfloat16),
        grads,
        (((1,), (1,)), ((), ())),
        preferred_element_type=jnp.float32,
    )
    mine = lax.dynamic_slice_in_dim(solution, lax.axis_index("cols") * own, own, axis=1)
    return (mine, scores * width ** (-0.5))


def solution(mesh):
    placed = (P(("rows", "cols"), None), P(None, "cols"))
    return jax.shard_map(
        per_device,
        mesh=mesh,
        in_specs=placed,
        out_specs=(P(None, "cols"), P(None, ("rows", "cols"))),
        check_vma=False,
    )
```

profile of v0, /device:TPU:0, one launch (start us, length us, event | category | flops | bytes accessed | tf_op | source)
XLA Modules:
  0.0 261.7 jit_solution(16199284651384448593)
XLA Ops:
  7.2 0.0 all-gather.2.cloned.1.call-start
  7.2 0.7 all-gather.2.cloned.1.call-update
  7.9 0.0 all-reduce.2.cloned.1.call-start
  7.9 50.0 %all-gather.2.cloned.1.call-done = f32[64,8192]{1,0:T(8,128)} async-done(((f32[64,2048]{1,0:T(8,128)}), f32[64,8192]{1,0:T(8,128)}) %all-gather.2.cloned.1.call-update) | async-done | bytes 2097168 | tf_op jit(solution)/shard_map/all_gather | solution.py:13
  58.0 9.7 %fusion = f32[64,8192]{1,0:T(8,128)} fusion(bf16[288,8192]{1,0:T(8,128)(2,1)} %param.2, f32[64,8192]{1,0:T(8,128)} %all-gather.2.cloned.1.call-done), kind=kOutput, calls=%fused_computation.11 | convolution fusion | flops 604522496 | bytes 8912896 | tf_op jit(solution)/shard_map/dot_general | solution.py:24
  67.6 0.0 copy-start
  67.6 0.0 all-reduce.2.cloned.1.call-update
  67.7 133.7 %all-reduce.2.cloned.1.call-done = f32[64,8192]{1,0:T(8,128)} async-done(((f32[64,8192]{1,0:T(8,128)}), f32[64,8192]{1,0:T(8,128)}) %all-reduce.2.cloned.1.call-update) | async-done | bytes 2097168 | tf_op jit(solution)/shard_map/psum | solution.py:30
  201.4 0.0 copy-done
  201.4 0.0 copy-start.1
  201.4 2.3 multiply_reduce_fusion.2
  203.7 0.0 copy-start.2
  203.7 2.3 multiply_reduce_fusion.1
  206.1 0.0 copy-done.1
  206.1 0.0 copy-done.2
  206.1 0.0 slice-start
  206.1 1.8 multiply_reduce_fusion.4
  207.9 38.9 %psum.15 = f32[64]{0:T(128)S(1)} all-reduce(f32[64]{0:T(128)S(1)} %multiply_reduce_fusion.4), channel_id=1, replica_groups=mesh['rows'=8,'cols'=4] {'rows','cols'}, use_global_device_ids=true, to_apply=%region_5.0 | all-reduce | flops 64 | bytes 512 | tf_op jit(solution)/shard_map/psum | solution.py:37
  246.9 0.0 slice-start.1
  246.9 2.5 multiply_reduce_fusion
  249.4 2.3 multiply_add_fusion
  251.7 0.0 slice-done
  251.7 0.0 slice-done.1
  251.7 2.3 convolution_multiply_fusion
  254.0 0.8 constant_dynamic-slice_fusion
  (4 shorter events, 0.0 us)
Async XLA Ops:
  7.2 50.8 %all-gather.2.cloned.1.call-start = ((), (), s32[]{:S(2)}) async-start(), calls=%async_computation | async-start | bytes 2621440 | tf_op jit(solution)/shard_map/all_gather | solution.py:13
  7.9 193.5 %all-reduce.2.cloned.1.call-start = ((), (), s32[]{:S(2)}) async-start(), calls=%async_computation.1 | async-start | bytes 4194304 | tf_op jit(solution)/shard_map/psum | solution.py:30
  67.6 133.7 %copy-start = (f32[64,8192]{1,0:T(8,128)S(1)}, f32[64,8192]{1,0:T(8,128)}, u32[]{:S(2)}) copy-start(f32[64,8192]{1,0:T(8,128)} %all-gather.2.cloned.1.call-done) | copy-start | bytes 6291460
  201.4 4.7 %copy-start.1 = (bf16[288,8192]{1,0:T(8,128)(2,1)S(1)}, bf16[288,8192]{1,0:T(8,128)(2,1)}, u32[]{:S(2)}) copy-start(bf16[288,8192]{1,0:T(8,128)(2,1)} %param.2) | copy-start | bytes 14155780
  203.7 2.4 copy-start.2
  206.1 45.6 %slice-start = ((s8[4718592]{0:T(1024)(128)(4,1)}), s8[524288]{0:T(1024)(128)(4,1)S(1)}, s32[]{:S(2)}) async-start(s8[4718592]{0:T(1024)(128)(4,1)} %bitcast.8), calls=%async_computation.2 | async-start | bytes 1048576
  246.9 4.8 %slice-start.1 = ((s8[4718592]{0:T(1024)(128)(4,1)}), s8[4194304]{0:T(1024)(128)(4,1)S(1)}, s32[]{:S(2)}) async-start(s8[4718592]{0:T(1024)(128)(4,1)} %bitcast.8), calls=%async_computation.3 | async-start | bytes 8388608
Sparse Core Ops, SparseCore 0:
  9.5 48.3 all-gather.1
  67.8 133.5 all-reduce.1
where the time goes:
time: 262 us
  waiting for transfers between devices  184 us (70%)
  blocking collectives  38.9 us (15%)
  between operations  14.1 us (5%)
  matrix products  13.8 us (5%)
  other arithmetic  9.47 us (4%)
    psum x1, waiting for transfers between devices, per_device(): lax.psum(partial_value, ('rows', 'cols')) / n_total + damping * direction  134 us
    all_gather x1, waiting for transfers between devices, per_device(): direction = lax.all_gather(tests, 'cols', axis=1, tiled=True)  50 us
    psum x1, blocking collectives, per_device(): lax.psum(jnp.sum(proj * proj.astype(jnp.bfloat16).astype(jnp.float32), ax...  38.9 us
    dot_general x1, matrix products, per_device(): lax.dot_general(project(direction).astype(jnp.bfloat16), grads, (((0,), (...  9.67 us
  transfers between devices with their start and end apart: 2, of which 2 were waited for; matrix products, arithmetic and copies ran while one was open for 0% of the time, Pallas kernels for 0%

commit v1 on v0

--- a/solution.py
+++ b/solution.py
@@ -6,11 +6,32 @@
 damping = 0.5
 
 
+def collect(x, axis, dim):
+    devices, index, span = (lax.axis_size(axis), lax.axis_index(axis), x.shape[dim])
+    right = [(i, (i + 1) % devices) for i in range(devices)]
+    left = [(i, (i - 1) % devices) for i in range(devices)]
+    result = jnp.zeros((*x.shape[:dim], devices * span, *x.shape[dim + 1 :]), x.dtype)
+    result = lax.dynamic_update_slice_in_dim(result, x, index * span, axis=dim)
+    from_left = from_right = x
+    middle = devices // 2
+    for hop in range(1, middle + 1):
+        from_left = lax.ppermute(from_left, axis, right)
+        result = lax.dynamic_update_slice_in_dim(
+            result, from_left, (index - hop) % devices * span, axis=dim
+        )
+        if hop < devices - middle:
+            from_right = lax.ppermute(from_right, axis, left)
+            result = lax.dynamic_update_slice_in_dim(
+                result, from_right, (index + hop) % devices * span, axis=dim
+            )
+    return result
+
+
 def per_device(grads, tests):
     n_total = grads.shape[0] * lax.axis_size("rows") * lax.axis_size("cols")
     width = grads.shape[1]
     own = tests.shape[1]
-    direction = lax.all_gather(tests, "cols", axis=1, tiled=True)
+    direction = collect(tests, "cols", 1)
     norm_now = jnp.sum(direction * direction, axis=1)
 
     def project(d):

time: 262 us -> 253 us (0.966)
  waiting for transfers between devices: 184 us -> 167 us
  starting transfers between devices: 0.08 us -> 5.24 us
    all_gather x1 -> x0, waiting for transfers between devices: 50 us -> none  [per_device(): direction = lax.all_gather(tests, 'cols', axis=1, tiled=True)]
    ppermute x0 -> x3, waiting for transfers between devices: none -> 33.3 us  [the longest x2 23.5 us: collect(): from_left = lax.ppermute(from_left, axis, right)]
    ppermute x0 -> x3, starting transfers between devices: none -> 5.2 us  [the longest x2 3.11 us: collect(): from_left = lax.ppermute(from_left, axis, right)]
  transfers between devices with their start and end apart: 2 -> 4, of which waited for: 2 -> 4; matrix products, arithmetic and copies ran while one was open for 0% -> 1% of each run, Pallas kernels for 0% -> 0%
where the time goes in v1:
time: 253 us
  waiting for transfers between devices  167 us (66%)
  blocking collectives  39 us (15%)
  matrix products  15.7 us (6%)
  between operations  14.2 us (6%)
  other arithmetic  7.81 us (3%)
  starting transfers between devices  5.24 us (2%)
  local copies, waits for them, and re-layouts  3.22 us (1%)
    psum x1, waiting for transfers between devices, per_device(): lax.psum(partial_value, ('rows', 'cols')) / n_total + damping * direction  134 us
    psum x1, blocking collectives, per_device(): lax.psum(jnp.sum(proj * proj.astype(jnp.bfloat16).astype(jnp.float32), ax...  39 us
    ppermute x2, waiting for transfers between devices, collect(): from_left = lax.ppermute(from_left, axis, right)  23.5 us
    ppermute x1, waiting for transfers between devices, collect(): from_right = lax.ppermute(from_right, axis, left)  9.81 us
    dot_general x1, matrix products, per_device(): lax.dot_general(project(direction).astype(jnp.bfloat16), grads, (((0,), (...  9.23 us
  transfers between devices with their start and end apart: 4, of which 4 were waited for; matrix products, arithmetic and copies ran while one was open for 1% of the time, Pallas kernels for 0%

profile of v1, /device:TPU:0, one launch (start us, length us, event | category | flops | bytes accessed | tf_op | source)
XLA Modules:
  0.0 252.5 jit_solution(15144454892165701603)
XLA Ops:
  7.2 0.0 copy-start.1
  7.2 0.0 all-reduce.2.cloned.1.call-start
  7.2 3.1 %collective-permute-start = (f32[64,2048]{1,0:T(8,128)}, f32[64,2048]{1,0:T(8,128)S(1)}, u32[]{:S(2)}, u32[]{:S(2)}) collective-permute-start(f32[64,2048]{1,0:T(8,128)} %param.3), channel_id=1, source_target_pairs={{0,1},{1,2},{2,3},{3,0},{4,5},{5,6},{6,7},{7,4},{8,9},{9,10},{10,1... | collective-permute-start | bytes 1572872 | tf_op jit(solution)/shard_map/ppermute | solution.py:18
  10.3 2.1 collective-permute-start.1
  12.4 13.0 %collective-permute-done = f32[64,2048]{1,0:T(8,128)S(1)} collective-permute-done((f32[64,2048]{1,0:T(8,128)}, f32[64,2048]{1,0:T(8,128)S(1)}, u32[]{:S(2)}, u32[]{:S(2)}) %collective-permute-start) | collective-permute-done | bytes 524320 | tf_op jit(solution)/shard_map/ppermute | solution.py:18
  25.4 0.0 collective-permute-start.2
  25.4 0.1 broadcast_in_dim.2
  25.5 0.0 copy-done.1
  25.7 9.8 %collective-permute-done.1 = f32[64,2048]{1,0:T(8,128)} collective-permute-done((f32[64,2048]{1,0:T(8,128)}, f32[64,2048]{1,0:T(8,128)}, u32[]{:S(2)}, u32[]{:S(2)}) %collective-permute-start.1) | collective-permute-done | bytes 524320 | tf_op jit(solution)/shard_map/ppermute | solution.py:23
  35.5 1.1 constant_dynamic-update-slice_fusion.1
  36.6 10.5 %collective-permute-done.2 = f32[64,2048]{1,0:T(8,128)} collective-permute-done((f32[64,2048]{1,0:T(8,128)S(1)}, f32[64,2048]{1,0:T(8,128)}, u32[]{:S(2)}, u32[]{:S(2)}) %collective-permute-start.2) | collective-permute-done | bytes 524320 | tf_op jit(solution)/shard_map/ppermute | solution.py:18
  47.1 1.1 constant_dynamic-update-slice_fusion
  48.2 9.2 %fusion = f32[64,8192]{1,0:T(8,128)} fusion(bf16[288,8192]{1,0:T(8,128)(2,1)} %param.2, f32[64,8192]{1,0:T(8,128)S(1)} %constant_dynamic-update-slice_fusion), kind=kOutput, calls=%fused_computation.11 | convolution fusion | flops 604522496 | bytes 8912896 | tf_op jit(solution)/shard_map/dot_general | solution.py:45
  57.4 0.0 all-reduce.2.cloned.1.call-update
  57.4 134.0 %all-reduce.2.cloned.1.call-done = f32[64,8192]{1,0:T(8,128)} async-done(((f32[64,8192]{1,0:T(8,128)}), f32[64,8192]{1,0:T(8,128)}) %all-reduce.2.cloned.1.call-update) | async-done | bytes 2097168 | tf_op jit(solution)/shard_map/psum | solution.py:51
  191.5 0.0 copy-start
  191.5 2.3 multiply_reduce_fusion.2
  193.8 0.0 copy-done
  193.8 0.7 multiply_reduce_fusion.1
  194.5 0.0 slice-start
  194.5 4.2 %multiply_reduce_fusion.4 = f32[64]{0:T(128)S(1)} fusion(bf16[288,8192]{1,0:T(8,128)(2,1)} %param.2, f32[64,8192]{1,0:T(8,128)S(1)} %constant_dynamic-update-slice_fusion, f32[64,8192]{1,0:T(8,128)S(1)} %copy-done, f32[64]{0:T(128)S(1)} %div.32, f32[64]{0:T(128)S(1)} %div.31), kind=kOutput, calls=%fused_computation.15 | convolution fusion | flops 306257856 | bytes 8913664 | tf_op jit(solution)/shard_map/dot_general | solution.py:38
  198.7 39.0 %psum.15 = f32[64]{0:T(128)S(1)} all-reduce(f32[64]{0:T(128)S(1)} %multiply_reduce_fusion.4), channel_id=1, replica_groups=mesh['rows'=8,'cols'=4] {'rows','cols'}, use_global_device_ids=true, to_apply=%region_5.6 | all-reduce | flops 64 | bytes 512 | tf_op jit(solution)/shard_map/psum | solution.py:58
  237.7 0.0 slice-start.1
  237.7 2.5 multiply_reduce_fusion
  240.2 2.3 multiply_add_fusion
  242.5 0.0 slice-done
  242.5 0.0 slice-done.1
  242.6 2.3 convolution_multiply_fusion
  244.8 0.8 constant_dynamic-slice_fusion
  (6 shorter events, 0.1 us)
Async XLA Ops:
  7.2 18.4 %copy-start.1 = (f32[64,2048]{1,0:T(8,128)S(1)}, f32[64,2048]{1,0:T(8,128)}, u32[]{:S(2)}) copy-start(f32[64,2048]{1,0:T(8,128)} %param.3) | copy-start | bytes 1572868
  7.2 184.3 %all-reduce.2.cloned.1.call-start = ((), (), s32[]{:S(2)}) async-start(), calls=%async_computation | async-start | bytes 4194304 | tf_op jit(solution)/shard_map/psum | solution.py:51
  7.2 18.2 %collective-permute-start = (f32[64,2048]{1,0:T(8,128)}, f32[64,2048]{1,0:T(8,128)S(1)}, u32[]{:S(2)}, u32[]{:S(2)}) collective-permute-start(f32[64,2048]{1,0:T(8,128)} %param.3), channel_id=1, source_target_pairs={{0,1},{1,2},{2,3},{3,0},{4,5},{5,6},{6,7},{7,4},{8,9},{9,10},{10,1... | collective-permute-start | bytes 1572872 | tf_op jit(solution)/shard_map/ppermute | solution.py:18
  10.3 25.2 %collective-permute-start.1 = (f32[64,2048]{1,0:T(8,128)}, f32[64,2048]{1,0:T(8,128)}, u32[]{:S(2)}, u32[]{:S(2)}) collective-permute-start(f32[64,2048]{1,0:T(8,128)} %param.3), channel_id=1, source_target_pairs={{0,3},{1,0},{2,1},{3,2},{4,7},{5,4},{6,5},{7,6},{8,11},{9,8},{10,9... | collective-permute-start | bytes 1572872 | tf_op jit(solution)/shard_map/ppermute | solution.py:23
  25.4 21.7 %collective-permute-start.2 = (f32[64,2048]{1,0:T(8,128)S(1)}, f32[64,2048]{1,0:T(8,128)}, u32[]{:S(2)}, u32[]{:S(2)}) collective-permute-start(f32[64,2048]{1,0:T(8,128)S(1)} %collective-permute-done), channel_id=1, source_target_pairs={{0,1},{1,2},{2,3},{3,0},{4,5},{5,6},{6,7},{7,4},{8,9},{9,10},{10,1... | collective-permute-start | bytes 1572872 | tf_op jit(solution)/shard_map/ppermute | solution.py:18
  191.5 2.3 copy-start
  194.5 48.0 %slice-start = ((s8[4718592]{0:T(1024)(128)(4,1)}), s8[524288]{0:T(1024)(128)(4,1)S(1)}, s32[]{:S(2)}) async-start(s8[4718592]{0:T(1024)(128)(4,1)} %bitcast.8), calls=%async_computation.1 | async-start | bytes 1048576
  237.7 4.8 %slice-start.1 = ((s8[4718592]{0:T(1024)(128)(4,1)}), s8[4194304]{0:T(1024)(128)(4,1)S(1)}, s32[]{:S(2)}) async-start(s8[4718592]{0:T(1024)(128)(4,1)} %bitcast.8), calls=%async_computation.2 | async-start | bytes 8388608
Sparse Core Ops, SparseCore 0:
  57.6 133.8 all-reduce.1
